TPU v7x, 128 devices: a whole 4x4x4 slice. The times are simulated.
128 devices in a mesh: sn: 32 (over x, y, core), rhs: 4 (over z).
Axes of the slice: x: 4, y: 4, z: 4, core: 2. Of those that a mesh axis runs over, the one named last changes fastest.
Arguments:
- rhs_leaf: float32 [1024, 256, 128], P('sn', 'rhs'), may hold values from -6 to 6
- rhs_top: float32 [32, 256, 128], P('sn', 'rhs'), may hold values from -6 to 6
- leaf_blocks: float32 [1024, 3, 128, 128], P('sn', None, 'rhs'), may hold values from -0.078125 to 0.078125
- leaf_dinv: float32 [1024, 128, 128], P('sn', 'rhs')
- leaf_struct: int32 [1024, 3], P('sn'), may hold values from 1 to 63, as said below
- top_blocks: float32 [32, 32, 128, 128], P(None, 'sn', 'rhs'), may hold values from -0.1875 to 0.1875
- top_dinv: float32 [32, 128, 128], P('sn', 'rhs')
Outputs:
- leaf_solution: float32 [1024, 256, 128], P('sn', 'rhs')
- top_solution: float32 [32, 256, 128], P('sn', 'rhs')
Inputs may be any that keep to these rules, and one draw needn't show every extreme that they name: `leaf_struct`: subtree d hangs below top supernode a = 4 * (d // 4). Row d * 32 + s names 3 distinct ancestors of leaf supernode s of subtree d: a value v < 32 is supernode v of the same subtree, with v > s; a value 32 + k is a top supernode k on a's path to the root, that is k = a or the factor holds top block (k, a). Column 0 is the elimination tree parent: s + 1, except for the subtree's last supernode, whose parent is 32 + a.
All inputs are finite; a program needn't handle non-finite values.
Results may differ from a plain program's by a relative error of at most 0.00018.
Values sent between devices are 32-bit elements; how exact they have to be, the bound alone decides.
A program may use at most 64 MiB of HBM per device.

v0:
```python
import jax
import jax.numpy as jnp
from jax import lax
from jax.sharding import PartitionSpec as P

highest = lax.Precision.HIGHEST


def top_levels(count):
    levels = count.bit_length()
    index = jnp.arange(count, dtype=jnp.int32)
    depth_of = jnp.zeros((count,), jnp.int32)
    span = jnp.ones((count,), jnp.int32)
    for place in range(levels):
        hit = ((index + 1) % 2 ** (place + 1) == 0).astype(jnp.int32)
        depth_of = depth_of + hit
        span = span + hit * 2**place
    row_index = index[:, None]
    col_index = index[None, :]
    keep = (col_index < row_index) & (col_index >= row_index + 1 - span[:, None])
    return (depth_of, keep.astype(jnp.float32))


def leaf_forward(top_total, rhs_part, blocks, inverses, struct):
    leaf_total = rhs_part.shape[0]
    updates = jnp.zeros((leaf_total + top_total,) + rhs_part.shape[1:], jnp.float32)
    values = jnp.zeros(rhs_part.shape, jnp.float32)

    def advance(position, state_pair):
        updates, values = state_pair
        source = lax.dynamic_index_in_dim(rhs_part, position, 0, False) - lax.dynamic_index_in_dim(
            updates, position, 0, False
        )
        solved = jnp.einsum(
            "ck,ik->ci",
            source,
            lax.dynamic_index_in_dim(inverses, position, 0, False),
            precision=highest,
        )
        targets = lax.dynamic_index_in_dim(struct, position, 0, False)
        outgoing = jnp.einsum(
            "ck,rik->rci",
            solved,
            lax.dynamic_index_in_dim(blocks, position, 0, False),
            precision=highest,
        )
        updates = updates.at[targets].add(outgoing)
        values = lax.dynamic_update_index_in_dim(values, solved, position, 0)
        return (updates, values)

    updates, values = lax.fori_loop(0, leaf_total, advance, (updates, values))
    return (values, updates[leaf_total:])


def leaf_backward(forward_values, blocks, inverses, struct, top_values):
    leaf_total = forward_values.shape[0]
    solution_buffer = jnp.concatenate([jnp.zeros_like(forward_values), top_values], axis=0)

    def retreat(offset, solution_buffer):
        position = leaf_total - 1 - offset
        targets = lax.dynamic_index_in_dim(struct, position, 0, False)
        ancestors = jnp.take(solution_buffer, targets, axis=0)
        summed = jnp.einsum(
            "rci,rik->ck",
            ancestors,
            lax.dynamic_index_in_dim(blocks, position, 0, False),
            precision=highest,
        )
        own_rhs = lax.dynamic_index_in_dim(forward_values, position, 0, False)
        solved = jnp.einsum(
            "ci,ik->ck",
            own_rhs - summed,
            lax.dynamic_index_in_dim(inverses, position, 0, False),
            precision=highest,
        )
        return lax.dynamic_update_index_in_dim(solution_buffer, solved, position, 0)

    solution_buffer = lax.fori_loop(0, leaf_total, retreat, solution_buffer)
    return solution_buffer[:leaf_total]


def forward_by_rows(top_source, masked_rows, own_inverse, my_level, levels, pull_values):
    forward_own = jnp.zeros_like(top_source)
    for level in range(levels):
        if level == 0:
            pulled = jnp.zeros_like(top_source)
        else:
            gathered = pull_values(forward_own[None])
            pulled = jnp.einsum("jck,jik->ci", gathered, masked_rows, precision=highest)
        candidate = jnp.einsum("ck,ik->ci", top_source - pulled, own_inverse, precision=highest)
        forward_own = jnp.where(my_level == level, candidate, forward_own)
    return forward_own


def backward_by_rows(forward_own, masked_rows, own_inverse, my_level, levels, sum_terms):
    backward_own = jnp.zeros_like(forward_own)
    pushed = jnp.zeros_like(forward_own)
    for level in range(levels - 1, -1, -1):
        candidate = jnp.einsum("ci,ik->ck", forward_own - pushed, own_inverse, precision=highest)
        backward_own = jnp.where(my_level == level, candidate, backward_own)
        if level > 0:
            sender = (my_level == level).astype(jnp.float32)
            outgoing = (
                jnp.einsum("ci,tik->tck", backward_own, masked_rows, precision=highest) * sender
            )
            pushed = pushed + sum_terms(outgoing)[0]
    return backward_own


def local(rhs_leaf, rhs_top, leaf_blocks, leaf_dinv, leaf_struct, top_blocks, top_dinv):
    blocks, inverses, top_cols, top_inverse = (
        lax.all_gather(leaf_blocks, "rhs", axis=2, tiled=True),
        lax.all_gather(leaf_dinv, "rhs", axis=1, tiled=True),
        lax.all_gather(top_blocks, "rhs", axis=2, tiled=True),
        lax.all_gather(top_dinv, "rhs", axis=1, tiled=True),
    )
    top_total = top_cols.shape[0]
    levels = top_total.bit_length()
    my_index = lax.axis_index("sn")
    depth_of, keep = top_levels(top_total)
    my_level = lax.dynamic_index_in_dim(depth_of, my_index, 0, False)
    own_inverse = top_inverse[0]
    forward_leaf, leaf_updates = leaf_forward(top_total, rhs_leaf, blocks, inverses, leaf_struct)
    own_update = lax.psum_scatter(leaf_updates, "sn", scatter_dimension=0, tiled=True)
    top_source = rhs_top[0] - own_update[0]
    keep_row = lax.dynamic_index_in_dim(keep, my_index, 0, False)
    row_blocks = lax.all_to_all(top_cols, "sn", split_axis=0, concat_axis=1, tiled=True)
    masked_rows = row_blocks[0] * keep_row[:, None, None]
    forward_own = forward_by_rows(
        top_source,
        masked_rows,
        own_inverse,
        my_level,
        levels,
        lambda stacked: lax.all_gather(stacked, "sn", axis=0, tiled=True),
    )
    backward_own = backward_by_rows(
        forward_own,
        masked_rows,
        own_inverse,
        my_level,
        levels,
        lambda stacked: lax.psum_scatter(stacked, "sn", scatter_dimension=0, tiled=True),
    )
    all_top = lax.all_gather(backward_own[None], "sn", axis=0, tiled=True)
    leaf_solution = leaf_backward(forward_leaf, blocks, inverses, leaf_struct, all_top)
    return (leaf_solution, backward_own[None])


def solution(mesh):
    return jax.shard_map(
        local,
        mesh=mesh,
        in_specs=(
            P("sn", "rhs", None),
            P("sn", "rhs", None),
            P("sn", None, "rhs", None),
            P("sn", "rhs", None),
            P("sn", None),
            P(None, "sn", "rhs", None),
            P("sn", "rhs", None),
        ),
        out_specs=(P("sn", "rhs", None), P("sn", "rhs", None)),
        check_vma=False,
    )
```

profile of v0, /device:TPU:1, one launch (start us, length us, event | category | flops | bytes accessed | tf_op | source)
XLA Modules:
  0.0 1077.8 jit_solution(17331218211384969366)
XLA Ops:
  9.5 34.2 %all-gather.18.cloned.1.call-done = f32[32,128,128]{2,1,0:T(8,128)} async-done(((f32[32,32,128]{2,1,0:T(8,128)}), f32[32,128,128]{2,1,0:T(8,128)}) %all-gather.18.cloned.1.call-update) | async-done | bytes 2097168 | tf_op jit(solution)/shard_map/all_gather | solution.py:113
  43.7 67.4 %all-gather.16.cloned.1.call-done = f32[32,3,128,128]{3,2,1,0:T(8,128)} async-done(((f32[32,3,32,128]{3,2,1,0:T(8,128)}), f32[32,3,128,128]{3,2,1,0:T(8,128)}) %all-gather.16.cloned.1.call-update) | async-done | bytes 6291472 | tf_op jit(solution)/shard_map/all_gather | solution.py:112
  111.4 100.6 %while.30 = (s32[]{:T(128)}, f32[64,64,128]{2,1,0:T(8,128)S(1)}, f32[32,64,128]{2,1,0:T(8,128)S(1)}, s32[32,3]{1,0:T(8,128)S(1)}, f32[32,3,128,128]{3,2,1,0:T(8,...) while((s32[]{:T(128)}, f32[64,64,128]{2,1,0:T(8,128)S(1)}, ...), condition=%wide.region_2.3_spmd, body=%wide.region_0.2_spmd.sunk | while | flops 50364424 | bytes 821373 | solution.py:51
  121.9 1.3 convolution_bitcast_fusion.9
  137.7 1.3 convolution_bitcast_fusion.9
  214.5 9.0 all_gather.32
  223.5 10.7 all-to-all-start
  234.3 55.7 %reduce-scatter.7.cloned.1.call-done = f32[1,64,128]{2,1,0:T(8,128)} async-done(((f32[32,64,128]{2,1,0:T(8,128)}), f32[1,64,128]{2,1,0:T(8,128)}) %reduce-scatter.7.cloned.1.call-update) | async-done | bytes 32784 | tf_op jit(solution)/shard_map/reduce_scatter | solution.py:124
  293.6 42.9 %all-gather.22.cloned.1.call-done = f32[2048,128]{1,0:T(8,128)} async-done(((f32[64,128]{1,0:T(8,128)}), f32[2048,128]{1,0:T(8,128)}) %all-gather.22.cloned.1.call-update) | async-done | bytes 1048592 | tf_op jit(solution)/shard_map/all_gather | solution.py:135
  336.6 3.6 fusion.36
  341.8 41.2 %all-gather.24.cloned.1.call-done = f32[2048,128]{1,0:T(8,128)} async-done(((f32[64,128]{1,0:T(8,128)}), f32[2048,128]{1,0:T(8,128)}) %all-gather.24.cloned.1.call-update) | async-done | bytes 1048592 | tf_op jit(solution)/shard_map/all_gather | solution.py:135
  383.0 3.6 fusion.35
  388.2 41.2 %all-gather.26.cloned.1.call-done = f32[2048,128]{1,0:T(8,128)} async-done(((f32[64,128]{1,0:T(8,128)}), f32[2048,128]{1,0:T(8,128)}) %all-gather.26.cloned.1.call-update) | async-done | bytes 1048592 | tf_op jit(solution)/shard_map/all_gather | solution.py:135
  429.4 3.6 fusion.34
  434.6 41.2 %all-gather.28.cloned.1.call-done = f32[2048,128]{1,0:T(8,128)} async-done(((f32[64,128]{1,0:T(8,128)}), f32[2048,128]{1,0:T(8,128)}) %all-gather.28.cloned.1.call-update) | async-done | bytes 1048592 | tf_op jit(solution)/shard_map/all_gather | solution.py:135
  475.9 3.6 fusion.33
  481.3 41.0 %all-gather.30.cloned.1.call-done = f32[2048,128]{1,0:T(8,128)} async-done(((f32[64,128]{1,0:T(8,128)}), f32[2048,128]{1,0:T(8,128)}) %all-gather.30.cloned.1.call-update) | async-done | bytes 1048592 | tf_op jit(solution)/shard_map/all_gather | solution.py:135
  522.3 3.6 fusion.32
  526.3 2.4 fusion.31
  528.8 75.1 %reduce-scatter.9.cloned.1.call-done = f32[1,64,128]{2,1,0:T(8,128)} async-done(((f32[32,64,128]{2,1,0:T(8,128)}), f32[1,64,128]{2,1,0:T(8,128)}) %reduce-scatter.9.cloned.1.call-update) | async-done | bytes 32784 | tf_op jit(solution)/shard_map/reduce_scatter | solution.py:143
  604.9 2.4 fusion.30
  607.4 77.8 %reduce-scatter.11.cloned.1.call-done = f32[1,64,128]{2,1,0:T(8,128)} async-done(((f32[32,64,128]{2,1,0:T(8,128)}), f32[1,64,128]{2,1,0:T(8,128)}) %reduce-scatter.11.cloned.1.call-update) | async-done | bytes 32784 | tf_op jit(solution)/shard_map/reduce_scatter | solution.py:143
  686.1 2.4 fusion.29
  688.6 77.6 %reduce-scatter.13.cloned.1.call-done = f32[1,64,128]{2,1,0:T(8,128)} async-done(((f32[32,64,128]{2,1,0:T(8,128)}), f32[1,64,128]{2,1,0:T(8,128)}) %reduce-scatter.13.cloned.1.call-update) | async-done | bytes 32784 | tf_op jit(solution)/shard_map/reduce_scatter | solution.py:143
  767.2 2.4 fusion.28
  769.6 77.8 %reduce-scatter.15.cloned.1.call-done = f32[1,64,128]{2,1,0:T(8,128)} async-done(((f32[32,64,128]{2,1,0:T(8,128)}), f32[1,64,128]{2,1,0:T(8,128)}) %reduce-scatter.15.cloned.1.call-update) | async-done | bytes 32784 | tf_op jit(solution)/shard_map/reduce_scatter | solution.py:143
  848.4 2.4 fusion.27
  850.9 77.5 %reduce-scatter.17.cloned.1.call-done = f32[1,64,128]{2,1,0:T(8,128)} async-done(((f32[32,64,128]{2,1,0:T(8,128)}), f32[1,64,128]{2,1,0:T(8,128)}) %reduce-scatter.17.cloned.1.call-update) | async-done | bytes 32784 | tf_op jit(solution)/shard_map/reduce_scatter | solution.py:143
  928.4 1.6 convolution_select_fusion
  930.0 45.2 %all-gather.32.cloned.1.call-done = f32[2048,128]{1,0:T(8,128)} async-done(((f32[64,128]{1,0:T(8,128)}), f32[2048,128]{1,0:T(8,128)}) %all-gather.32.cloned.1.call-update) | async-done | bytes 1048592 | tf_op jit(solution)/shard_map/all_gather | solution.py:145
  975.2 1.5 concatenate.3
  976.6 93.5 %while.31 = (s32[]{:T(128)}, f32[64,64,128]{2,1,0:T(8,128)S(1)}, f32[32,64,128]{2,1,0:T(8,128)S(1)}, s32[32,3]{1,0:T(8,128)S(1)}, f32[32,3,128,128]{3,2,1,0:T(8,...) while((s32[]{:T(128)}, f32[64,64,128]{2,1,0:T(8,128)S(1)}, ...), condition=%wide.region_10.11_spmd, body=%wide.region_9.10_spmd.sunk | while | flops 50365472 | bytes 693510 | solution.py:78
  (395 shorter events, 204.5 us)
Async XLA Ops:
  7.2 2.3 copy-start.10
  7.2 36.5 %all-gather.18.cloned.1.call-start = ((), (), s32[]{:S(2)}) async-start(), calls=%async_computation.8 | async-start | bytes 2621440 | tf_op jit(solution)/shard_map/all_gather | solution.py:113
  7.9 103.2 %all-gather.16.cloned.1.call-start = ((), (), s32[]{:S(2)}) async-start(), calls=%async_computation.7 | async-start | bytes 7864320 | tf_op jit(solution)/shard_map/all_gather | solution.py:112
  8.7 214.9 %all-gather.20.cloned.1.call-start = ((), (), s32[]{:S(2)}) async-start(), calls=%async_computation.10 | async-start | bytes 2621440 | tf_op jit(solution)/shard_map/all_gather | solution.py:114
  9.4 280.6 %reduce-scatter.7.cloned.1.call-start = ((), (), s32[]{:S(2)}) async-start(), calls=%async_computation.9 | async-start | bytes 1081344 | tf_op jit(solution)/shard_map/reduce_scatter | solution.py:124
  212.0 2.5 copy-start.9
  223.5 66.4 %copy-start.8 = (f32[1,64,128]{2,1,0:T(8,128)S(1)}, f32[1,64,128]{2,1,0:T(8,128)}, u32[]{:S(2)}) copy-start(f32[1,64,128]{2,1,0:T(8,128)} %param.12) | copy-start | bytes 98308
  223.5 70.1 %all-to-all-start = ((f32[32,1,128,128]{3,2,1,0:T(8,128)}), f32[32,1,128,128]{3,2,1,0:T(8,128)S(1)}, u32[]{:S(2)}, u32[]{:S(2)}) async-start(f32[32,1,128,128]{3,2,1,0:T(8,128)} %all-gather.20.cloned.1.call-done), calls=%async_computation.1 | async-start | bytes 4194304 | tf_op jit(solution)/shard_map/all_to_all | solution.py:127
  234.2 102.3 %all-gather.22.cloned.1.call-start = ((), (), s32[]{:S(2)}) async-start(), calls=%async_computation.16 | async-start | bytes 1081344 | tf_op jit(solution)/shard_map/all_gather | solution.py:135
  291.6 48.6 %copy-start.4 = (f32[64,128]{1,0:T(8,128)S(1)}, f32[64,128]{1,0:T(8,128)}, u32[]{:S(2)}) copy-start(f32[64,128]{1,0:T(8,128)} %convolution_select_fusion.11) | copy-start | bytes 98308
  291.6 91.4 %all-gather.24.cloned.1.call-start = ((), (), s32[]{:S(2)}) async-start(), calls=%async_computation.17 | async-start | bytes 1081344 | tf_op jit(solution)/shard_map/all_gather | solution.py:135
  341.0 45.6 %copy-start.1 = (f32[64,128]{1,0:T(8,128)S(1)}, f32[64,128]{1,0:T(8,128)}, u32[]{:S(2)}) copy-start(f32[64,128]{1,0:T(8,128)} %convolution_select_fusion.10) | copy-start | bytes 98308
  341.0 88.4 %all-gather.26.cloned.1.call-start = ((), (), s32[]{:S(2)}) async-start(), calls=%async_computation.18 | async-start | bytes 1081344 | tf_op jit(solution)/shard_map/all_gather | solution.py:135
  387.4 45.6 %copy-start.2 = (f32[64,128]{1,0:T(8,128)S(1)}, f32[64,128]{1,0:T(8,128)}, u32[]{:S(2)}) copy-start(f32[64,128]{1,0:T(8,128)} %convolution_select_fusion.9) | copy-start | bytes 98308
  387.5 88.4 %all-gather.28.cloned.1.call-start = ((), (), s32[]{:S(2)}) async-start(), calls=%async_computation.19 | async-start | bytes 1081344 | tf_op jit(solution)/shard_map/all_gather | solution.py:135
  433.9 45.6 %copy-start.3 = (f32[64,128]{1,0:T(8,128)S(1)}, f32[64,128]{1,0:T(8,128)}, u32[]{:S(2)}) copy-start(f32[64,128]{1,0:T(8,128)} %convolution_select_fusion.8) | copy-start | bytes 98308
  433.9 88.4 %all-gather.30.cloned.1.call-start = ((), (), s32[]{:S(2)}) async-start(), calls=%async_computation.20 | async-start | bytes 1081344 | tf_op jit(solution)/shard_map/all_gather | solution.py:135
  480.3 45.6 %copy-start = (f32[64,128]{1,0:T(8,128)S(1)}, f32[64,128]{1,0:T(8,128)}, u32[]{:S(2)}) copy-start(f32[64,128]{1,0:T(8,128)} %convolution_select_fusion.7) | copy-start | bytes 98308
  480.3 123.6 %reduce-scatter.9.cloned.1.call-start = ((), (), s32[]{:S(2)}) async-start(), calls=%async_computation.11 | async-start | bytes 1081344 | tf_op jit(solution)/shard_map/reduce_scatter | solution.py:143
  528.8 156.4 %reduce-scatter.11.cloned.1.call-start = ((), (), s32[]{:S(2)}) async-start(), calls=%async_computation.12 | async-start | bytes 1081344 | tf_op jit(solution)/shard_map/reduce_scatter | solution.py:143
  604.9 80.3 %copy-start.5 = (f32[1,64,128]{2,1,0:T(8,128)S(1)}, f32[1,64,128]{2,1,0:T(8,128)}, u32[]{:S(2)}) copy-start(f32[1,64,128]{2,1,0:T(8,128)} %reduce-scatter.9.cloned.1.call-done) | copy-start | bytes 98308
  607.3 158.9 %reduce-scatter.13.cloned.1.call-start = ((), (), s32[]{:S(2)}) async-start(), calls=%async_computation.13 | async-start | bytes 1081344 | tf_op jit(solution)/shard_map/reduce_scatter | solution.py:143
  686.1 80.1 %copy-start.6 = (f32[1,64,128]{2,1,0:T(8,128)S(1)}, f32[1,64,128]{2,1,0:T(8,128)}, u32[]{:S(2)}) copy-start(f32[1,64,128]{2,1,0:T(8,128)} %reduce-scatter.11.cloned.1.call-done) | copy-start | bytes 98308
  688.5 158.9 %reduce-scatter.15.cloned.1.call-start = ((), (), s32[]{:S(2)}) async-start(), calls=%async_computation.14 | async-start | bytes 1081344 | tf_op jit(solution)/shard_map/reduce_scatter | solution.py:143
  769.6 158.8 %reduce-scatter.17.cloned.1.call-start = ((), (), s32[]{:S(2)}) async-start(), calls=%async_computation.15 | async-start | bytes 1081344 | tf_op jit(solution)/shard_map/reduce_scatter | solution.py:143
  848.4 80.0 %copy-start.7 = (f32[1,64,128]{2,1,0:T(8,128)S(1)}, f32[1,64,128]{2,1,0:T(8,128)}, u32[]{:S(2)}) copy-start(f32[1,64,128]{2,1,0:T(8,128)} %reduce-scatter.15.cloned.1.call-done) | copy-start | bytes 98308
  850.8 124.3 %all-gather.32.cloned.1.call-start = ((), (), s32[]{:S(2)}) async-start(), calls=%async_computation.21 | async-start | bytes 1081344 | tf_op jit(solution)/shard_map/all_gather | solution.py:145
Sparse Core Ops, SparseCore 0:
  9.6 34.0 all-gather.17
  45.4 65.7 all-gather.15
  112.8 31.4 all-gather.19
  213.3 76.6 reduce-scatter.6
  292.6 43.8 all-gather.21
  341.1 41.7 all-gather.23
  387.6 41.7 all-gather.25
  434.0 41.7 all-gather.27
  480.5 41.7 all-gather.29
  528.9 75.0 reduce-scatter.8
  608.0 77.0 reduce-scatter.10
  689.1 77.0 reduce-scatter.12
  770.3 77.1 reduce-scatter.14
  851.4 77.0 reduce-scatter.16
  931.1 44.0 all-gather.31
where the time goes:
time: 1080 us
  waiting for transfers between devices  798 us (74%)
  matrix products  189 us (18%)
  other arithmetic  25.3 us (2%)
  local copies, waits for them, and re-layouts  23 us (2%)
  between operations  18.4 us (2%)
  starting transfers between devices  11.5 us (1%)
    reduce_scatter x5, waiting for transfers between devices, local(): lax.psum_scatter(stacked, 'sn', scatter_dimension=0, tiled=True)  386 us
    all_gather x5, waiting for transfers between devices, local(): lax.all_gather(stacked, 'sn', axis=0, tiled=True)  208 us
    all_gather x1, waiting for transfers between devices, local(): lax.all_gather(leaf_blocks, 'rhs', axis=2, tiled=True)  67.4 us
    reduce_scatter x1, waiting for transfers between devices, local(): lax.psum_scatter(leaf_updates, 'sn', scatter_dimension=0, tiled=True)  55.7 us
    all_gather x1, waiting for transfers between devices, local(): all_top = lax.all_gather(backward_own[None], 'sn', axis=0, tiled=True)  45.2 us
    dot_general x32, matrix products, advance(): jnp.einsum('ck,rik->rci', solved, lax.dynamic_index_in_dim(blocks, positi...  41.9 us
    dot_general x32, matrix products, retreat(): jnp.einsum('rci,rik->ck', ancestors, lax.dynamic_index_in_dim(blocks, pos...  39.4 us
    dot_general x32, matrix products, advance(): jnp.einsum('ck,ik->ci', source, lax.dynamic_index_in_dim(inverses, positi...  35.3 us
  transfers between devices with their start and end apart: 16, of which 14 were waited for; matrix products, arithmetic and copies ran while one was open for 10% of the time, Pallas kernels for 0%

commit v1 on v0

--- a/solution.py
+++ b/solution.py
@@ -4,6 +4,13 @@
 from jax.sharding import PartitionSpec as P
 
 highest = lax.Precision.HIGHEST
+
+
+def all_by_exchange(shard, name, along):
+    n_dev = lax.axis_size(name)
+    tiles = jnp.stack([shard for _ in range(n_dev)])
+    tiles = lax.all_to_all(tiles, name, split_axis=0, concat_axis=0)
+    return jnp.concatenate(tiles, axis=along)
 
 
 def top_levels(count):
@@ -132,7 +139,7 @@
         own_inverse,
         my_level,
         levels,
-        lambda stacked: lax.all_gather(stacked, "sn", axis=0, tiled=True),
+        lambda stacked: all_by_exchange(stacked, "sn", 0),
     )
     backward_own = backward_by_rows(
         forward_own,

time: 1080 us -> 1140 us (1.056)
  waiting for transfers between devices: 798 us -> 702 us
  local copies, waits for them, and re-layouts: 23 us -> 84.8 us
  other arithmetic: 25.3 us -> 69 us
  matrix products: 189 us -> 220 us
  starting transfers between devices: 11.5 us -> 31.5 us
    all_gather x5 -> x0, waiting for transfers between devices: 208 us -> none  [local(): lax.all_gather(stacked, 'sn', axis=0, tiled=True)]
    all_to_all x0 -> x5, waiting for transfers between devices: none -> 79.8 us  [all_by_exchange(): tiles = lax.all_to_all(tiles, name, split_axis=0, concat_axis=0)]
    gather x32, local copies, waits for them, and re-layouts: 17.8 us -> 68.5 us  [retreat(): ancestors = jnp.take(solution_buffer, targets, axis=0)]
    scatter-add x32, other arithmetic: 21.6 us -> 65.5 us  [advance(): updates = updates.at[targets].add(outgoing)]
    all_gather x1, waiting for transfers between devices: 0.01 us -> 34.2 us  [local(): lax.all_gather(top_blocks, 'rhs', axis=2, tiled=True)]
    all_to_all x0 -> x5, starting transfers between devices: none -> 23.2 us  [all_by_exchange(): tiles = lax.all_to_all(tiles, name, split_axis=0, concat_axis=0)]
    dot_general x32, matrix products: 35.3 us -> 55.5 us  [advance(): jnp.einsum('ck,ik->ci', source, lax.dynamic_index_in_dim(inverses, positi...]
    dot_general x32, matrix products: 32.9 us -> 52.6 us  [retreat(): jnp.einsum('ci,ik->ck', own_rhs - summed, lax.dynamic_index_in_dim(invers...]
  transfers between devices with their start and end apart: 16 -> 16, of which waited for: 14 -> 15; matrix products, arithmetic and copies ran while one was open for 10% -> 15% of each run, Pallas kernels for 0% -> 0%
where the time goes in v1:
time: 1140 us
  waiting for transfers between devices  702 us (62%)
  matrix products  220 us (19%)
  local copies, waits for them, and re-layouts  84.8 us (7%)
  other arithmetic  69 us (6%)
  starting transfers between devices  31.5 us (3%)
  between operations  18.4 us (2%)
    reduce_scatter x5, waiting for transfers between devices, local(): lax.psum_scatter(stacked, 'sn', scatter_dimension=0, tiled=True)  382 us
    all_to_all x5, waiting for transfers between devices, all_by_exchange(): tiles = lax.all_to_all(tiles, name, split_axis=0, concat_axis=0)  79.8 us
    gather x32, local copies, waits for them, and re-layouts, retreat(): ancestors = jnp.take(solution_buffer, targets, axis=0)  68.5 us
    all_gather x1, waiting for transfers between devices, local(): lax.all_gather(leaf_blocks, 'rhs', axis=2, tiled=True)  67.4 us
    reduce_scatter x1, waiting for transfers between devices, local(): lax.psum_scatter(leaf_updates, 'sn', scatter_dimension=0, tiled=True)  66.4 us
    scatter-add x32, other arithmetic, advance(): updates = updates.at[targets].add(outgoing)  65.5 us
    dot_general x32, matrix products, advance(): jnp.einsum('ck,ik->ci', source, lax.dynamic_index_in_dim(inverses, positi...  55.5 us
    dot_general x32, matrix products, retreat(): jnp.einsum('ci,ik->ck', own_rhs - summed, lax.dynamic_index_in_dim(invers...  52.6 us
  transfers between devices with their start and end apart: 16, of which 15 were waited for; matrix products, arithmetic and copies ran while one was open for 15% of the time, Pallas kernels for 0%

profile of v1, /device:TPU:1, one launch (start us, length us, event | category | flops | bytes accessed | tf_op | source)
XLA Modules:
  0.0 1135.5 jit_solution(7036593655733570670)
XLA Ops:
  9.5 34.2 %all-gather.10.cloned.1.call-done = f32[32,1,128,128]{3,2,1,0:T(8,128)} async-done(((f32[32,1,32,128]{3,2,1,0:T(8,128)}), f32[32,1,128,128]{3,2,1,0:T(8,128)}) %all-gather.10.cloned.1.call-update) | async-done | bytes 2097168 | tf_op jit(solution)/shard_map/all_gather | solution.py:121
  43.7 7.7 all-to-all-start.1
  51.5 24.8 %all-gather.8.cloned.1.call-done = f32[32,128,128]{2,1,0:T(8,128)} async-done(((f32[32,32,128]{2,1,0:T(8,128)}), f32[32,128,128]{2,1,0:T(8,128)}) %all-gather.8.cloned.1.call-update) | async-done | bytes 2097168 | tf_op jit(solution)/shard_map/all_gather | solution.py:120
  76.3 67.4 %all-gather.6.cloned.1.call-done = f32[32,3,128,128]{3,2,1,0:T(8,128)} async-done(((f32[32,3,32,128]{3,2,1,0:T(8,128)}), f32[32,3,128,128]{3,2,1,0:T(8,128)}) %all-gather.6.cloned.1.call-update) | async-done | bytes 6291472 | tf_op jit(solution)/shard_map/all_gather | solution.py:119
  145.3 163.1 %while.30 = (s32[]{:T(128)}, f32[64,64,128]{2,1,0:T(8,128)}, f32[32,64,128]{2,1,0:T(8,128)}, s32[32,3]{1,0:T(8,128)S(1)}, f32[32,3,128,128]{3,2,1,0:T(8,128)}, /...) while((s32[]{:T(128)}, f32[64,64,128]{2,1,0:T(8,128)}, f32[32,64,128]{2,1,0:T(8,128)}, ...), condition=%wide.region_2.3_spmd, body=%wide.region_0.2_spmd.sunk | while | flops 50364424 | bytes 820873 | solution.py:58
  308.4 2.4 slice.6
  312.1 9.0 all_gather.17
  321.1 66.4 %reduce-scatter.7.cloned.1.call-done = f32[1,64,128]{2,1,0:T(8,128)} async-done(((f32[32,64,128]{2,1,0:T(8,128)}), f32[1,64,128]{2,1,0:T(8,128)}) %reduce-scatter.7.cloned.1.call-update) | async-done | bytes 32784 | tf_op jit(solution)/shard_map/reduce_scatter | solution.py:131
  389.7 7.5 all-to-all-start
  399.1 15.0 %all-to-all-done = f32[32,1,64,128]{3,2,1,0:T(8,128)S(1)} async-done(((f32[32,1,64,128]{3,2,1,0:T(8,128)}), f32[32,1,64,128]{3,2,1,0:T(8,128)S(1)}, u32[]{:S(2)}, u32[]{:S(2)}) %all-to-all-start) | async-done | bytes 1048608 | tf_op jit(solution)/shard_map/all_to_all | solution.py:12
  417.9 3.9 all-to-all-start.2
  422.4 16.3 %all-to-all-done.2 = f32[32,1,64,128]{3,2,1,0:T(8,128)S(1)} async-done(((f32[32,1,64,128]{3,2,1,0:T(8,128)}), f32[32,1,64,128]{3,2,1,0:T(8,128)S(1)}, u32[]{:S(2)}, u32[]{:S(2)}) %all-to-all-start.2) | async-done | bytes 1048608 | tf_op jit(solution)/shard_map/all_to_all | solution.py:12
  442.5 3.9 all-to-all-start.3
  447.0 16.3 %all-to-all-done.3 = f32[32,1,64,128]{3,2,1,0:T(8,128)S(1)} async-done(((f32[32,1,64,128]{3,2,1,0:T(8,128)}), f32[32,1,64,128]{3,2,1,0:T(8,128)S(1)}, u32[]{:S(2)}, u32[]{:S(2)}) %all-to-all-start.3) | async-done | bytes 1048608 | tf_op jit(solution)/shard_map/all_to_all | solution.py:12
  467.1 3.9 all-to-all-start.4
  471.7 16.3 %all-to-all-done.4 = f32[32,1,64,128]{3,2,1,0:T(8,128)S(1)} async-done(((f32[32,1,64,128]{3,2,1,0:T(8,128)}), f32[32,1,64,128]{3,2,1,0:T(8,128)S(1)}, u32[]{:S(2)}, u32[]{:S(2)}) %all-to-all-start.4) | async-done | bytes 1048608 | tf_op jit(solution)/shard_map/all_to_all | solution.py:12
  487.9 2.3 fusion.75
  491.7 3.9 all-to-all-start.5
  496.5 16.0 %all-to-all-done.5 = f32[32,1,64,128]{3,2,1,0:T(8,128)S(1)} async-done(((f32[32,1,64,128]{3,2,1,0:T(8,128)}), f32[32,1,64,128]{3,2,1,0:T(8,128)S(1)}, u32[]{:S(2)}, u32[]{:S(2)}) %all-to-all-start.5) | async-done | bytes 1048608 | tf_op jit(solution)/shard_map/all_to_all | solution.py:12
  515.3 2.5 fusion.48
  517.9 73.7 %reduce-scatter.9.cloned.1.call-done = f32[1,64,128]{2,1,0:T(8,128)} async-done(((f32[32,64,128]{2,1,0:T(8,128)}), f32[1,64,128]{2,1,0:T(8,128)}) %reduce-scatter.9.cloned.1.call-update) | async-done | bytes 32784 | tf_op jit(solution)/shard_map/reduce_scatter | solution.py:150
  592.5 2.5 fusion.50
  595.1 77.1 %reduce-scatter.11.cloned.1.call-done = f32[1,64,128]{2,1,0:T(8,128)} async-done(((f32[32,64,128]{2,1,0:T(8,128)}), f32[1,64,128]{2,1,0:T(8,128)}) %reduce-scatter.11.cloned.1.call-update) | async-done | bytes 32784 | tf_op jit(solution)/shard_map/reduce_scatter | solution.py:150
  673.2 2.5 fusion.52
  675.7 77.2 %reduce-scatter.13.cloned.1.call-done = f32[1,64,128]{2,1,0:T(8,128)} async-done(((f32[32,64,128]{2,1,0:T(8,128)}), f32[1,64,128]{2,1,0:T(8,128)}) %reduce-scatter.13.cloned.1.call-update) | async-done | bytes 32784 | tf_op jit(solution)/shard_map/reduce_scatter | solution.py:150
  753.9 2.5 fusion.54
  756.5 77.2 %reduce-scatter.15.cloned.1.call-done = f32[1,64,128]{2,1,0:T(8,128)} async-done(((f32[32,64,128]{2,1,0:T(8,128)}), f32[1,64,128]{2,1,0:T(8,128)}) %reduce-scatter.15.cloned.1.call-update) | async-done | bytes 32784 | tf_op jit(solution)/shard_map/reduce_scatter | solution.py:150
  834.6 2.5 fusion.56
  837.2 77.2 %reduce-scatter.17.cloned.1.call-done = f32[1,64,128]{2,1,0:T(8,128)} async-done(((f32[32,64,128]{2,1,0:T(8,128)}), f32[1,64,128]{2,1,0:T(8,128)}) %reduce-scatter.17.cloned.1.call-update) | async-done | bytes 32784 | tf_op jit(solution)/shard_map/reduce_scatter | solution.py:150
  916.0 45.2 %all-gather.12.cloned.1.call-done = f32[2048,128]{1,0:T(8,128)} async-done(((f32[64,128]{1,0:T(8,128)}), f32[2048,128]{1,0:T(8,128)}) %all-gather.12.cloned.1.call-update) | async-done | bytes 1048592 | tf_op jit(solution)/shard_map/all_gather | solution.py:152
  961.1 2.9 concatenate.3
  964.0 162.4 %while.31 = (s32[]{:T(128)}, f32[64,64,128]{2,1,0:T(8,128)}, f32[32,64,128]{2,1,0:T(8,128)}, s32[32,3]{1,0:T(8,128)S(1)}, f32[32,3,128,128]{3,2,1,0:T(8,128)}, /...) while((s32[]{:T(128)}, f32[64,64,128]{2,1,0:T(8,128)}, ...), condition=%wide.region_10.11_spmd, body=%wide.region_9.10_spmd.sunk | while | flops 50365472 | bytes 693518 | solution.py:85
  (385 shorter events, 356.2 us)
Async XLA Ops:
  7.2 2.2 copy-start.5
  7.2 36.5 %all-gather.10.cloned.1.call-start = ((), (), s32[]{:S(2)}) async-start(), calls=%async_computation.15 | async-start | bytes 2621440 | tf_op jit(solution)/shard_map/all_gather | solution.py:121
  7.9 68.4 %all-gather.8.cloned.1.call-start = ((), (), s32[]{:S(2)}) async-start(), calls=%async_computation.13 | async-start | bytes 2621440 | tf_op jit(solution)/shard_map/all_gather | solution.py:120
  8.7 135.0 %all-gather.6.cloned.1.call-start = ((), (), s32[]{:S(2)}) async-start(), calls=%async_computation.12 | async-start | bytes 7864320 | tf_op jit(solution)/shard_map/all_gather | solution.py:119
  43.7 344.8 %all-to-all-start.1 = ((f32[32,1,128,128]{3,2,1,0:T(8,128)}), f32[32,1,128,128]{3,2,1,0:T(8,128)S(1)}, u32[]{:S(2)}, u32[]{:S(2)}) async-start(f32[32,1,128,128]{3,2,1,0:T(8,128)} %all-gather.10.cloned.1.call-done), calls=%async_computation.2 | async-start | bytes 4194304 | tf_op jit(solution)/shard_map/all_to_all | solution.py:134
  51.4 336.1 %reduce-scatter.7.cloned.1.call-start = ((), (), s32[]{:S(2)}) async-start(), calls=%async_computation.14 | async-start | bytes 1081344 | tf_op jit(solution)/shard_map/reduce_scatter | solution.py:131
  308.4 3.7 copy-start.4
  308.4 79.0 %copy-start.3 = (f32[1,64,128]{2,1,0:T(8,128)S(1)}, f32[1,64,128]{2,1,0:T(8,128)}, u32[]{:S(2)}) copy-start(f32[1,64,128]{2,1,0:T(8,128)} %param.12) | copy-start | bytes 98308
  389.7 24.4 %all-to-all-start = ((f32[32,1,64,128]{3,2,1,0:T(8,128)}), f32[32,1,64,128]{3,2,1,0:T(8,128)S(1)}, u32[]{:S(2)}, u32[]{:S(2)}) async-start(f32[32,1,64,128]{3,2,1,0:T(8,128)} %stack.15), calls=%async_computation.1 | async-start | bytes 2097152 | tf_op jit(solution)/shard_map/all_to_all | solution.py:12
  417.9 20.8 %all-to-all-start.2 = ((f32[32,1,64,128]{3,2,1,0:T(8,128)}), f32[32,1,64,128]{3,2,1,0:T(8,128)S(1)}, u32[]{:S(2)}, u32[]{:S(2)}) async-start(f32[32,1,64,128]{3,2,1,0:T(8,128)} %stack.16), calls=%async_computation.3 | async-start | bytes 2097152 | tf_op jit(solution)/shard_map/all_to_all | solution.py:12
  442.5 20.8 %all-to-all-start.3 = ((f32[32,1,64,128]{3,2,1,0:T(8,128)}), f32[32,1,64,128]{3,2,1,0:T(8,128)S(1)}, u32[]{:S(2)}, u32[]{:S(2)}) async-start(f32[32,1,64,128]{3,2,1,0:T(8,128)} %stack.17), calls=%async_computation.4 | async-start | bytes 2097152 | tf_op jit(solution)/shard_map/all_to_all | solution.py:12
  467.1 20.8 %all-to-all-start.4 = ((f32[32,1,64,128]{3,2,1,0:T(8,128)}), f32[32,1,64,128]{3,2,1,0:T(8,128)S(1)}, u32[]{:S(2)}, u32[]{:S(2)}) async-start(f32[32,1,64,128]{3,2,1,0:T(8,128)} %stack.18), calls=%async_computation.5 | async-start | bytes 2097152 | tf_op jit(solution)/shard_map/all_to_all | solution.py:12
  491.7 20.8 %all-to-all-start.5 = ((f32[32,1,64,128]{3,2,1,0:T(8,128)}), f32[32,1,64,128]{3,2,1,0:T(8,128)S(1)}, u32[]{:S(2)}, u32[]{:S(2)}) async-start(f32[32,1,64,128]{3,2,1,0:T(8,128)} %stack.19), calls=%async_computation.6 | async-start | bytes 2097152 | tf_op jit(solution)/shard_map/all_to_all | solution.py:12
  495.6 95.9 %reduce-scatter.9.cloned.1.call-start = ((), (), s32[]{:S(2)}) async-start(), calls=%async_computation.16 | async-start | bytes 1081344 | tf_op jit(solution)/shard_map/reduce_scatter | solution.py:150
  517.8 154.4 %reduce-scatter.11.cloned.1.call-start = ((), (), s32[]{:S(2)}) async-start(), calls=%async_computation.17 | async-start | bytes 1081344 | tf_op jit(solution)/shard_map/reduce_scatter | solution.py:150
  592.5 79.7 %copy-start = (f32[1,64,128]{2,1,0:T(8,128)S(1)}, f32[1,64,128]{2,1,0:T(8,128)}, u32[]{:S(2)}) copy-start(f32[1,64,128]{2,1,0:T(8,128)} %reduce-scatter.9.cloned.1.call-done) | copy-start | bytes 98308
  595.0 157.9 %reduce-scatter.13.cloned.1.call-start = ((), (), s32[]{:S(2)}) async-start(), calls=%async_computation.18 | async-start | bytes 1081344 | tf_op jit(solution)/shard_map/reduce_scatter | solution.py:150
  673.2 79.8 %copy-start.1 = (f32[1,64,128]{2,1,0:T(8,128)S(1)}, f32[1,64,128]{2,1,0:T(8,128)}, u32[]{:S(2)}) copy-start(f32[1,64,128]{2,1,0:T(8,128)} %reduce-scatter.11.cloned.1.call-done) | copy-start | bytes 98308
  675.7 158.0 %reduce-scatter.15.cloned.1.call-start = ((), (), s32[]{:S(2)}) async-start(), calls=%async_computation.19 | async-start | bytes 1081344 | tf_op jit(solution)/shard_map/reduce_scatter | solution.py:150
  756.4 158.0 %reduce-scatter.17.cloned.1.call-start = ((), (), s32[]{:S(2)}) async-start(), calls=%async_computation.20 | async-start | bytes 1081344 | tf_op jit(solution)/shard_map/reduce_scatter | solution.py:150
  834.6 79.8 %copy-start.2 = (f32[1,64,128]{2,1,0:T(8,128)S(1)}, f32[1,64,128]{2,1,0:T(8,128)}, u32[]{:S(2)}) copy-start(f32[1,64,128]{2,1,0:T(8,128)} %reduce-scatter.15.cloned.1.call-done) | copy-start | bytes 98308
  837.1 124.0 %all-gather.12.cloned.1.call-start = ((), (), s32[]{:S(2)}) async-start(), calls=%async_computation.21 | async-start | bytes 1081344 | tf_op jit(solution)/shard_map/all_gather | solution.py:152
Sparse Core Ops, SparseCore 0:
  9.6 34.0 all-gather.9
  45.4 30.8 all-gather.7
  77.9 65.7 all-gather.5
  311.0 76.4 reduce-scatter.6
  517.9 73.5 reduce-scatter.8
  595.1 77.0 reduce-scatter.10
  675.8 77.0 reduce-scatter.12
  756.5 77.0 reduce-scatter.14
  837.2 77.0 reduce-scatter.16
  917.0 44.0 all-gather.11
